TPU v7x, 32 devices: a whole 2x2x4 slice. The times are simulated.
32 devices in a mesh: groups: 2 (over x), dap: 16 (over z, y, core).
Axes of the slice: x: 2, y: 2, z: 4, core: 2. Of those that a mesh axis runs over, the one named last changes fastest.
Arguments:
- homolog_tensor: bfloat16 [128, 32, 256], P(('groups', 'dap')), parts along dimension 0, may hold values from -1 to 1
- couple_tensor: bfloat16 [64, 32, 128], P(('groups', 'dap')), parts along dimension 0, may hold values from -6 to 6
- horizontal_drop_filter: int32 [64, 256], P('groups'), parts along dimension 0, may hold values 0 or 1
- couple_offset_matrix: bfloat16 [128, 8], replicated, may hold values from -0.29882812 to 0.29882812
- horizontal_attend_matrix: bfloat16 [256, 1024], replicated, may hold values from -0.375 to 0.375
- horizontal_exit_matrix: bfloat16 [256, 256], replicated, may hold values from -0.375 to 0.375
- vertical_attend_matrix: bfloat16 [256, 1024], replicated, may hold values from -0.375 to 0.375
- vertical_exit_matrix: bfloat16 [256, 256], replicated, may hold values from -0.375 to 0.375
- averaged_product_flanks: bfloat16 [256, 64], replicated, may hold values from -0.375 to 0.375
- averaged_product_exit: bfloat16 [1024, 128], replicated, may hold values from -1 to 1
Outputs:
- alignment_output: bfloat16 [128, 32, 256], P('groups', 'dap'), parts along dimension 0
- pair_output_state: bfloat16 [64, 32, 128], P(('groups', 'dap')), parts along dimension 0
There are 2 independent parts, one for each index of `groups`. A program takes and returns all parts, laid end to end along the dimension named above; an argument that names none is the same for every part. Nothing has to cross between parts.
All inputs are finite; a program needn't handle non-finite values.
Results may differ from a plain program's by a relative error of at most 0.012.
Values may be sent and summed in bfloat16 or wider, within the bound.
No kernel may reach another device: no remote copies, remote signals or barrier semaphores. Data moves between devices by JAX's collectives and lax.ppermute only.
A program may use at most 64 MiB of HBM per device.

v0:
```python
import jax
import jax.numpy as jnp
from jax import lax
from jax.sharding import PartitionSpec as P

HEAD_NUMBER = 8
HEAD_WIDTH = 32
FACTOR_FEATURES = 32


def standardise_features(values):
    values = values.astype(jnp.float32)
    center = values - jnp.mean(values, axis=-1, keepdims=True)
    spread = jnp.mean(center * center, axis=-1, keepdims=True)
    return center * lax.rsqrt(spread + 1e-05)


def attend(normed, w_qkvg, w_out, bias):
    batch, length = (normed.shape[0], normed.shape[1])
    proj = jnp.einsum("blc,cf->blf", normed, w_qkvg, preferred_element_type=jnp.float32)
    proj = proj.reshape(batch, length, 4, HEAD_NUMBER, HEAD_WIDTH)
    query = (proj[:, :, 0] * HEAD_WIDTH ** (-0.5)).astype(jnp.bfloat16)
    keys = proj[:, :, 1].astype(jnp.bfloat16)
    values = proj[:, :, 2].astype(jnp.bfloat16)
    gate = proj[:, :, 3]
    if bias is None:
        bias = jnp.zeros((HEAD_NUMBER, length, length), jnp.bfloat16)

    def one_head(items):
        qh, kh, vh, bh = items
        scores = jnp.einsum("bid,bjd->bij", qh, kh, preferred_element_type=jnp.float32)
        scores = scores + bh.astype(jnp.float32)[None]
        weights = jax.nn.softmax(scores, axis=-1).astype(jnp.bfloat16)
        return jnp.einsum("bij,bjd->bid", weights, vh, preferred_element_type=jnp.float32)

    heads = lax.map(
        one_head,
        (jnp.moveaxis(query, 2, 0), jnp.moveaxis(keys, 2, 0), jnp.moveaxis(values, 2, 0), bias),
    )
    heads = jnp.moveaxis(heads, 0, 2)
    gated = (
        (jax.nn.sigmoid(gate) * heads)
        .astype(jnp.bfloat16)
        .reshape(batch, length, HEAD_NUMBER * HEAD_WIDTH)
    )
    return jnp.einsum("blk,kc->blc", gated, w_out, preferred_element_type=jnp.float32)


def shards(
    homolog_tensor,
    couple_tensor,
    horizontal_drop_filter,
    couple_offset_matrix,
    horizontal_attend_matrix,
    horizontal_exit_matrix,
    vertical_attend_matrix,
    vertical_exit_matrix,
    averaged_product_flanks,
    averaged_product_exit,
):
    normed_pair = standardise_features(couple_tensor).astype(jnp.bfloat16)
    own_bias = jnp.einsum(
        "ijz,zh->hij", normed_pair, couple_offset_matrix, preferred_element_type=jnp.float32
    ).astype(jnp.bfloat16)
    bias = lax.all_gather(own_bias, "dap", axis=1, tiled=True)
    starting_answer = standardise_features(homolog_tensor).astype(jnp.bfloat16)
    perform_refresh = attend(
        starting_answer, horizontal_attend_matrix, horizontal_exit_matrix, bias
    )
    homolog_later = (
        homolog_tensor.astype(jnp.float32)
        + horizontal_drop_filter.astype(jnp.float32) * (1.0 / 0.9) * perform_refresh
    ).astype(jnp.bfloat16)
    incoming_blocks = lax.all_to_all(homolog_later, "dap", split_axis=1, concat_axis=0, tiled=True)
    column_layout = jnp.swapaxes(incoming_blocks, 0, 1)
    perform_refresh = attend(
        standardise_features(column_layout).astype(jnp.bfloat16),
        vertical_attend_matrix,
        vertical_exit_matrix,
        None,
    )
    alignment_output = jnp.swapaxes(
        (column_layout.astype(jnp.float32) + perform_refresh).astype(jnp.bfloat16), 0, 1
    )
    final_result = standardise_features(alignment_output).astype(jnp.bfloat16)
    factors = jnp.einsum(
        "sic,cf->sif", final_result, averaged_product_flanks, preferred_element_type=jnp.float32
    )
    left = factors[..., :FACTOR_FEATURES].astype(jnp.bfloat16)
    right = factors[..., FACTOR_FEATURES:].astype(jnp.bfloat16)
    total = left.shape[0]
    own_rows = left.shape[1]
    whole = lax.all_gather(right, "dap", axis=1, tiled=True)
    outer = jnp.einsum("sic,sjd->ijcd", left, whole, preferred_element_type=jnp.float32) / total
    outer = outer.astype(jnp.bfloat16).reshape(
        own_rows, whole.shape[1], FACTOR_FEATURES * FACTOR_FEATURES
    )
    change = jnp.einsum(
        "ijk,kz->ijz", outer, averaged_product_exit, preferred_element_type=jnp.float32
    )
    pair_output_state = (couple_tensor.astype(jnp.float32) + change).astype(jnp.bfloat16)
    return (alignment_output, pair_output_state)


def solution(mesh):
    placed = (
        P(("groups", "dap"), None, None),
        P(("groups", "dap"), None, None),
        P("groups", None),
        P(),
        P(),
        P(),
        P(),
        P(),
        P(),
        P(),
    )
    return jax.shard_map(
        shards,
        mesh=mesh,
        in_specs=placed,
        out_specs=(P("groups", "dap", None), P(("groups", "dap"), None, None)),
        check_vma=False,
    )
```

profile of v0, /device:TPU:0, one launch (start us, length us, event | category | flops | bytes accessed | tf_op | source)
XLA Modules:
  0.0 80.2 jit_solution(14656866743398978957)
XLA Ops:
  0.6 1.0 %convert_reduce_fusion = f32[4,32]{1,0:T(4,128)S(1)} fusion(bf16[4,32,256]{2,1,0:T(8,128)(2,1)} %param.14), kind=kLoop, calls=%fused_computation.81 | loop fusion | flops 65408 | bytes 66048 | tf_op jit(solution)/shard_map/reduce_sum | solution.py:13
  1.7 1.0 %fusion.104 = f32[4,32]{1,0:T(4,128)S(1)} fusion(bf16[4,32,256]{2,1,0:T(8,128)(2,1)} %param.14, f32[4,32]{1,0:T(4,128)S(1)} %broadcast_multiply_fusion), kind=kLoop, calls=%fused_computation.88 | loop fusion | flops 130944 | bytes 66560 | tf_op jit(solution)/shard_map/reduce_sum | solution.py:14
  2.7 1.1 %fusion.87 = f32[4,32,1024]{2,1,0:T(8,128)S(1)} fusion(bf16[256,1024]{1,0:T(8,128)(2,1)S(1)} %copy-done, bf16[4,32,256]{2,1,0:T(8,128)(2,1)} %param.14, f32[4,32]{1,0:T(4,128)S(1)} %add_rsqrt_fusion, f32[4,32]{1,0:T(4,128)S(1)} %broadcast_multiply_fusion), kind=kOutput, calls=%fused_computation.63 | convolution fusion | flops 67239936 | bytes 1115136 | tf_op jit(solution)/shard_map/blc,cf->blf/dot_general | solution.py:20
  3.8 0.7 reshape.102
  4.5 2.6 %copy.41 = f32[4,32,4,8,32]{4,1,0,3,2:T(8,128)} copy(f32[4,32,4,8,32]{4,3,2,1,0:T(8,128)S(1)} %reshape.102) | data formatting | bytes 1048576 | tf_op jit(solution)/shard_map/reshape | solution.py:21
  7.1 2.2 %copy.76 = bf16[4,32,4,8,32]{4,1,0,3,2:T(8,128)(2,1)} copy(f32[4,32,4,8,32]{4,3,2,1,0:T(8,128)S(1)} %reshape.102) | data formatting | bytes 786432 | tf_op jit(solution)/shard_map/reshape | solution.py:21
  9.3 1.1 %fusion.90 = bf16[8,4,32,32]{3,2,1,0:T(8,128)(2,1)S(1)} fusion(f32[4,32,4,8,32]{4,1,0,3,2:T(8,128)} %copy.41), kind=kLoop, calls=%fused_computation.66 | loop fusion | flops 65536 | bytes 196608 | tf_op jit(solution)/shard_map/transpose | solution.py:38
  10.4 1.1 %slice_bitcast_fusion = (bf16[8,4,32,32]{3,2,1,0:T(8,128)(2,1)S(1)}, bf16[8,4,32,32]{3,2,1,0:T(8,128)(2,1)S(1)}) fusion(bf16[4,32,4,8,32]{4,1,0,3,2:T(8,128)(2,1)} %copy.76), kind=kLoop, calls=%fused_computation.75 | loop fusion | bytes 262144 | tf_op jit(solution)/shard_map/transpose | solution.py:38
  11.6 0.2 fusion.121
  11.7 0.2 fusion.78
  11.9 23.3 %all_gather.6 = bf16[8,32,32]{2,0,1:T(8,128)(2,1)S(1)} all-gather(bf16[8,2,32]{2,0,1:T(8,128)(2,1)S(1)} %fusion.78), channel_id=1, replica_groups=mesh['groups'=2,'dap'=16] {'dap'}, dimensions={1}, use_global_device_ids=true | all-gather | bytes 17408 | tf_op jit(solution)/shard_map/all_gather | solution.py:65
  35.2 0.1 copy.44
  35.4 4.3 %while.20 = (s32[]{:T(128)}, f32[8,4,32,32]{3,2,1,0:T(8,128)S(1)}, bf16[8,4,32,32]{3,2,1,0:T(8,128)(2,1)S(1)}, bf16[8,4,32,32]{3,2,1,0:T(8,128)(2,1)S(1)}, bf16[...) while((s32[]{:T(128)}, f32[8,4,32,32]{3,2,1,0:T(8,128)S(1)}, ...), condition=%wide.region_7.8_spmd, body=%wide.region_4.7_spmd.sunk | while | flops 816320 | bytes 274001 | solution.py:36
  35.4 0.2 fusion.161
  35.6 0.3 fusion.162
  36.0 0.2 fusion.161
  36.1 0.3 fusion.162
  36.5 0.2 fusion.161
  36.7 0.3 fusion.162
  37.0 0.2 fusion.161
  37.2 0.3 fusion.162
  37.6 0.2 fusion.161
  37.7 0.3 fusion.162
  38.1 0.2 fusion.161
  38.3 0.3 fusion.162
  38.6 0.2 fusion.161
  38.8 0.3 fusion.162
  39.1 0.2 fusion.161
  39.3 0.3 fusion.162
  39.7 1.3 %fusion.89 = bf16[4,32,8,32]{3,1,0,2:T(8,128)(2,1)S(1)} fusion(f32[8,4,32,32]{3,2,1,0:T(8,128)S(1)} %get-tuple-element.61, f32[4,32,4,8,32]{4,1,0,3,2:T(8,128)} %copy.41), kind=kLoop, calls=%fused_computation.65 | loop fusion | flops 163840 | bytes 327680 | tf_op jit(solution)/shard_map/convert_element_type | solution.py:43
  40.9 0.2 copy.45
  41.1 0.2 reshape.103
  41.3 0.2 fusion.76
  41.5 0.7 copy.46
  42.2 3.5 %all-to-all-start = ((bf16[4,32,256]{2,0,1:T(4,128)(2,1)}), bf16[4,32,256]{2,0,1:T(4,128)(2,1)S(1)}, u32[]{:S(2)}, u32[]{:S(2)}) async-start(bf16[4,32,256]{2,0,1:T(4,128)(2,1)} %copy.46), calls=%async_computation | async-start | bytes 131072 | tf_op jit(solution)/shard_map/all_to_all | solution.py:74
  45.7 6.8 %all-to-all-done = bf16[4,32,256]{2,0,1:T(4,128)(2,1)S(1)} async-done(((bf16[4,32,256]{2,0,1:T(4,128)(2,1)}), bf16[4,32,256]{2,0,1:T(4,128)(2,1)S(1)}, u32[]{:S(2)}, u32[]{:S(2)}) %all-to-all-start) | async-done | bytes 65568 | tf_op jit(solution)/shard_map/all_to_all | solution.py:74
  52.7 0.2 multiply_reduce_fusion
  52.9 0.4 fusion.85
  53.5 4.7 %while.21 = (s32[]{:T(128)}, f32[8,2,64,32]{2,3,0,1:T(8,128)S(1)}, bf16[8,2,64,32]{2,3,0,1:T(8,128)(2,1)S(1)}, bf16[8,2,64,32]{2,3,0,1:T(8,128)(2,1)S(1)}, bf16[8,2,64,32]{2,3,0,1:T(8,128)(2,1)S(1)}, /*index=5*/s32[]{:T(128)}) while((s32[]{:T(128)}, f32[8,2,64,32]{2,3,0,1:T(8,128)S(1)}, bf16[8,2,64,32]{2,3,0,1:T(8,128)(2,1)S(1)}, ...), condition=%wide.region_13.14_spmd, body=%wide.region_10.13_spmd.sunk | while | flops 1614080 | bytes 119365 | solution.py:36
  53.5 0.2 fusion.168
  53.8 0.3 fusion.169
  54.1 0.2 fusion.168
  54.4 0.3 fusion.169
  54.7 0.2 fusion.168
  55.0 0.3 fusion.169
  55.3 0.2 fusion.168
  55.6 0.3 fusion.169
  55.9 0.2 fusion.168
  56.1 0.3 fusion.169
  56.5 0.2 fusion.168
  56.7 0.3 fusion.169
  57.1 0.2 fusion.168
  57.3 0.3 fusion.169
  57.7 0.2 fusion.168
  57.9 0.3 fusion.169
  58.4 0.3 convert_reduce_fusion.1
  58.7 0.7 copy.55
  59.4 0.2 fusion.106
  59.6 0.2 convolution_convert_fusion
  59.8 18.5 %all_gather.7 = bf16[64,32,32]{0,2,1:T(8,128)(2,1)S(1)} all-gather(bf16[64,2,32]{0,2,1:T(8,128)(2,1)S(1)} %slice.54), channel_id=1, replica_groups=mesh['groups'=2,'dap'=16] {'dap'}, dimensions={1}, use_global_device_ids=true | all-gather | bytes 139264 | tf_op jit(solution)/shard_map/all_gather | solution.py:93
  78.3 0.3 fusion.72
  78.6 0.3 copy.54
  78.9 0.5 reshape.106
  79.5 0.8 fusion.77
  (48 shorter events, 0.6 us)
Async XLA Ops:
  0.6 2.0 %copy-start = (bf16[256,1024]{1,0:T(8,128)(2,1)S(1)}, bf16[256,1024]{1,0:T(8,128)(2,1)}, u32[]{:S(2)}) copy-start(bf16[256,1024]{1,0:T(8,128)(2,1)} %param.18) | copy-start | bytes 1572868
  7.1 4.4 %copy-start.4 = (bf16[2,32,128]{2,1,0:T(8,128)(2,1)S(1)}, bf16[2,32,128]{2,1,0:T(8,128)(2,1)}, u32[]{:S(2)}) copy-start(bf16[2,32,128]{2,1,0:T(8,128)(2,1)} %param.15) | copy-start | bytes 49156
  7.1 4.7 %copy-start.9 = (bf16[128,8]{0,1:T(8,128)(2,1)S(1)}, bf16[128,8]{0,1:T(8,128)(2,1)}, u32[]{:S(2)}) copy-start(bf16[128,8]{0,1:T(8,128)(2,1)} %param.17) | copy-start | bytes 6148
  35.4 5.9 %copy-start.7 = (s32[32,256]{1,0:T(8,128)S(1)}, s32[32,256]{1,0:T(8,128)}, u32[]{:S(2)}) copy-start(s32[32,256]{1,0:T(8,128)} %param.16) | copy-start | bytes 98308
  35.4 5.9 %copy-start.1 = (bf16[4,32,256]{2,1,0:T(8,128)(2,1)S(1)}, bf16[4,32,256]{2,1,0:T(8,128)(2,1)}, u32[]{:S(2)}) copy-start(bf16[4,32,256]{2,1,0:T(8,128)(2,1)} %param.14) | copy-start | bytes 196612
  35.4 5.9 %copy-start.6 = (bf16[256,256]{1,0:T(8,128)(2,1)S(1)}, bf16[256,256]{1,0:T(8,128)(2,1)}, u32[]{:S(2)}) copy-start(bf16[256,256]{1,0:T(8,128)(2,1)} %param.19) | copy-start | bytes 393220
  39.7 13.2 %copy-start.2 = (bf16[256,1024]{1,0:T(8,128)(2,1)S(1)}, bf16[256,1024]{1,0:T(8,128)(2,1)}, u32[]{:S(2)}) copy-start(bf16[256,1024]{1,0:T(8,128)(2,1)} %param.20) | copy-start | bytes 1572868
  42.2 10.4 %all-to-all-start = ((bf16[4,32,256]{2,0,1:T(4,128)(2,1)}), bf16[4,32,256]{2,0,1:T(4,128)(2,1)S(1)}, u32[]{:S(2)}, u32[]{:S(2)}) async-start(bf16[4,32,256]{2,0,1:T(4,128)(2,1)} %copy.46), calls=%async_computation | async-start | bytes 131072 | tf_op jit(solution)/shard_map/all_to_all | solution.py:74
  53.4 4.9 %copy-start.5 = (bf16[256,256]{1,0:T(8,128)(2,1)S(1)}, bf16[256,256]{1,0:T(8,128)(2,1)}, u32[]{:S(2)}) copy-start(bf16[256,256]{1,0:T(8,128)(2,1)} %param.21) | copy-start | bytes 393220
  53.5 6.1 %copy-start.8 = (bf16[256,64]{0,1:T(8,128)(2,1)S(1)}, bf16[256,64]{0,1:T(8,128)(2,1)}, u32[]{:S(2)}) copy-start(bf16[256,64]{0,1:T(8,128)(2,1)} %param.22) | copy-start | bytes 98308
  58.3 21.2 %copy-start.3 = (bf16[1024,128]{1,0:T(8,128)(2,1)S(1)}, bf16[1024,128]{1,0:T(8,128)(2,1)}, u32[]{:S(2)}) copy-start(bf16[1024,128]{1,0:T(8,128)(2,1)} %param.23) | copy-start | bytes 786436
where the time goes:
time: 80.6 us; the launch traced here: 80.2 us
  blocking collectives  41.8 us (52%)
  matrix products  12.4 us (15%)
  local copies, waits for them, and re-layouts  9.33 us (12%)
  waiting for transfers between devices  6.85 us (8%)
  other arithmetic  5.33 us (7%)
  starting transfers between devices  3.5 us (4%)
  between operations  0.95 us (1%)
    all_gather x1, blocking collectives, shards(): bias = lax.all_gather(own_bias, 'dap', axis=1, tiled=True)  23.3 us
    all_gather x1, blocking collectives, shards(): whole = lax.all_gather(right, 'dap', axis=1, tiled=True)  18.5 us
    all_to_all x1, waiting for transfers between devices, shards(): lax.all_to_all(homolog_later, 'dap', split_axis=1, concat_axis=0, tiled=T...  6.85 us
    dot_general x16, matrix products, one_head(): jnp.einsum('bij,bjd->bid', weights, vh, preferred_element_type=jnp.float32)  5.53 us
    reshape x3, local copies, waits for them, and re-layouts, attend(): proj = proj.reshape(batch, length, 4, HEAD_NUMBER, HEAD_WIDTH)  5.46 us
    all_to_all x1, starting transfers between devices, shards(): lax.all_to_all(homolog_later, 'dap', split_axis=1, concat_axis=0, tiled=T...  3.5 us
    sub x16, matrix products, one_head(): weights = jax.nn.softmax(scores, axis=-1).astype(jnp.bfloat16)  3.4 us
  transfers between devices with their start and end apart: 1, of which 1 were waited for; matrix products, arithmetic and copies ran while one was open for 0% of the time, Pallas kernels for 0%

commit v1 on v0

--- a/solution.py
+++ b/solution.py
@@ -90,7 +90,9 @@
     right = factors[..., FACTOR_FEATURES:].astype(jnp.bfloat16)
     total = left.shape[0]
     own_rows = left.shape[1]
-    whole = lax.all_gather(right, "dap", axis=1, tiled=True)
+    whole = jnp.concatenate(
+        lax.all_to_all(jnp.stack([right] * lax.axis_size("dap")), "dap", 0, 0), axis=1
+    )
     outer = jnp.einsum("sic,sjd->ijcd", left, whole, preferred_element_type=jnp.float32) / total
     outer = outer.astype(jnp.bfloat16).reshape(
         own_rows, whole.shape[1], FACTOR_FEATURES * FACTOR_FEATURES

time: 80.6 us -> 74.1 us (0.919)
  blocking collectives: 41.8 us -> 23.3 us
  waiting for transfers between devices: 6.85 us -> 14 us
  starting transfers between devices: 3.5 us -> 7.01 us
  local copies, waits for them, and re-layouts: 9.33 us -> 10.5 us
    all_gather x1 -> x0, blocking collectives: 18.5 us -> none  [shards(): whole = lax.all_gather(right, 'dap', axis=1, tiled=True)]
    all_to_all x0 -> x1, waiting for transfers between devices: none -> 7.17 us  [shards(): lax.all_to_all(jnp.stack([right] * lax.axis_size('dap')), 'dap', 0, 0)]
    all_to_all x0 -> x1, starting transfers between devices: none -> 3.51 us  [shards(): lax.all_to_all(jnp.stack([right] * lax.axis_size('dap')), 'dap', 0, 0)]
    unnamed x21 -> x24, local copies, waits for them, and re-layouts: 0.76 us -> 1.89 us
  transfers between devices with their start and end apart: 1 -> 2, of which waited for: 1 -> 2; matrix products, arithmetic and copies ran while one was open for 0% -> 1% of each run, Pallas kernels for 0% -> 0%
where the time goes in v1:
time: 74.1 us; the launch traced here: 73.6 us
  blocking collectives  23.3 us (31%)
  waiting for transfers between devices  14 us (19%)
  matrix products  12.4 us (17%)
  local copies, waits for them, and re-layouts  10.5 us (14%)
  starting transfers between devices  7.01 us (9%)
  other arithmetic  5.33 us (7%)
  between operations  0.99 us (1%)
    all_gather x1, blocking collectives, shards(): bias = lax.all_gather(own_bias, 'dap', axis=1, tiled=True)  23.3 us
    all_to_all x1, waiting for transfers between devices, shards(): lax.all_to_all(jnp.stack([right] * lax.axis_size('dap')), 'dap', 0, 0)  7.17 us
    all_to_all x1, waiting for transfers between devices, shards(): lax.all_to_all(homolog_later, 'dap', split_axis=1, concat_axis=0, tiled=T...  6.85 us
    dot_general x16, matrix products, one_head(): jnp.einsum('bij,bjd->bid', weights, vh, preferred_element_type=jnp.float32)  5.53 us
    reshape x3, local copies, waits for them, and re-layouts, attend(): proj = proj.reshape(batch, length, 4, HEAD_NUMBER, HEAD_WIDTH)  5.46 us
    all_to_all x1, starting transfers between devices, shards(): lax.all_to_all(jnp.stack([right] * lax.axis_size('dap')), 'dap', 0, 0)  3.51 us
    all_to_all x1, starting transfers between devices, shards(): lax.all_to_all(homolog_later, 'dap', split_axis=1, concat_axis=0, tiled=T...  3.5 us
    sub x16, matrix products, one_head(): weights = jax.nn.softmax(scores, axis=-1).astype(jnp.bfloat16)  3.4 us
  transfers between devices with their start and end apart: 2, of which 2 were waited for; matrix products, arithmetic and copies ran while one was open for 1% of the time, Pallas kernels for 0%

profile of v1, /device:TPU:0, one launch (start us, length us, event | category | flops | bytes accessed | tf_op | source)
XLA Modules:
  0.0 73.6 jit_solution(13600373186008178615)
XLA Ops:
  0.6 1.0 %convert_reduce_fusion = f32[4,32]{1,0:T(4,128)S(1)} fusion(bf16[4,32,256]{2,1,0:T(8,128)(2,1)} %param.14), kind=kLoop, calls=%fused_computation.80 | loop fusion | flops 65408 | bytes 66048 | tf_op jit(solution)/shard_map/reduce_sum | solution.py:13
  1.7 1.0 %fusion.103 = f32[4,32]{1,0:T(4,128)S(1)} fusion(bf16[4,32,256]{2,1,0:T(8,128)(2,1)} %param.14, f32[4,32]{1,0:T(4,128)S(1)} %broadcast_multiply_fusion), kind=kLoop, calls=%fused_computation.87 | loop fusion | flops 130944 | bytes 66560 | tf_op jit(solution)/shard_map/reduce_sum | solution.py:14
  2.7 1.1 %fusion.87 = f32[4,32,1024]{2,1,0:T(8,128)S(1)} fusion(bf16[256,1024]{1,0:T(8,128)(2,1)S(1)} %copy-done, bf16[4,32,256]{2,1,0:T(8,128)(2,1)} %param.14, f32[4,32]{1,0:T(4,128)S(1)} %add_rsqrt_fusion, f32[4,32]{1,0:T(4,128)S(1)} %broadcast_multiply_fusion), kind=kOutput, calls=%fused_computation.63 | convolution fusion | flops 67239936 | bytes 1115136 | tf_op jit(solution)/shard_map/blc,cf->blf/dot_general | solution.py:20
  3.8 0.7 reshape.110
  4.5 2.6 %copy.41 = f32[4,32,4,8,32]{4,1,0,3,2:T(8,128)} copy(f32[4,32,4,8,32]{4,3,2,1,0:T(8,128)S(1)} %reshape.110) | data formatting | bytes 1048576 | tf_op jit(solution)/shard_map/reshape | solution.py:21
  7.1 2.2 %copy.76 = bf16[4,32,4,8,32]{4,1,0,3,2:T(8,128)(2,1)} copy(f32[4,32,4,8,32]{4,3,2,1,0:T(8,128)S(1)} %reshape.110) | data formatting | bytes 786432 | tf_op jit(solution)/shard_map/reshape | solution.py:21
  9.3 1.1 %fusion.90 = bf16[8,4,32,32]{3,2,1,0:T(8,128)(2,1)S(1)} fusion(f32[4,32,4,8,32]{4,1,0,3,2:T(8,128)} %copy.41), kind=kLoop, calls=%fused_computation.66 | loop fusion | flops 65536 | bytes 196608 | tf_op jit(solution)/shard_map/transpose | solution.py:38
  10.4 1.1 %slice_bitcast_fusion = (bf16[8,4,32,32]{3,2,1,0:T(8,128)(2,1)S(1)}, bf16[8,4,32,32]{3,2,1,0:T(8,128)(2,1)S(1)}) fusion(bf16[4,32,4,8,32]{4,1,0,3,2:T(8,128)(2,1)} %copy.76), kind=kLoop, calls=%fused_computation.75 | loop fusion | bytes 262144 | tf_op jit(solution)/shard_map/transpose | solution.py:38
  11.7 0.2 fusion.78
  11.9 23.3 %all_gather.3 = bf16[8,32,32]{2,0,1:T(8,128)(2,1)S(1)} all-gather(bf16[8,2,32]{2,0,1:T(8,128)(2,1)S(1)} %fusion.78), channel_id=1, replica_groups=mesh['groups'=2,'dap'=16] {'dap'}, dimensions={1}, use_global_device_ids=true | all-gather | bytes 17408 | tf_op jit(solution)/shard_map/all_gather | solution.py:65
  35.4 4.3 %while.20 = (s32[]{:T(128)}, f32[8,4,32,32]{3,2,1,0:T(8,128)S(1)}, bf16[8,4,32,32]{3,2,1,0:T(8,128)(2,1)S(1)}, bf16[8,4,32,32]{3,2,1,0:T(8,128)(2,1)S(1)}, bf16[...) while((s32[]{:T(128)}, f32[8,4,32,32]{3,2,1,0:T(8,128)S(1)}, ...), condition=%wide.region_7.8_spmd, body=%wide.region_4.7_spmd.sunk | while | flops 816320 | bytes 274001 | solution.py:36
  35.4 0.2 fusion.161
  35.6 0.3 fusion.162
  36.0 0.2 fusion.161
  36.1 0.3 fusion.162
  36.5 0.2 fusion.161
  36.7 0.3 fusion.162
  37.0 0.2 fusion.161
  37.2 0.3 fusion.162
  37.6 0.2 fusion.161
  37.7 0.3 fusion.162
  38.1 0.2 fusion.161
  38.3 0.3 fusion.162
  38.6 0.2 fusion.161
  38.8 0.3 fusion.162
  39.1 0.2 fusion.161
  39.3 0.3 fusion.162
  39.7 1.3 %fusion.89 = bf16[4,32,8,32]{3,1,0,2:T(8,128)(2,1)S(1)} fusion(f32[8,4,32,32]{3,2,1,0:T(8,128)S(1)} %get-tuple-element.61, f32[4,32,4,8,32]{4,1,0,3,2:T(8,128)} %copy.41), kind=kLoop, calls=%fused_computation.65 | loop fusion | flops 163840 | bytes 327680 | tf_op jit(solution)/shard_map/convert_element_type | solution.py:43
  40.9 0.2 copy.45
  41.1 0.2 reshape.111
  41.3 0.2 fusion.76
  41.5 0.7 copy.46
  42.2 3.5 %all-to-all-start = ((bf16[4,32,256]{2,0,1:T(4,128)(2,1)}), bf16[4,32,256]{2,0,1:T(4,128)(2,1)S(1)}, u32[]{:S(2)}, u32[]{:S(2)}) async-start(bf16[4,32,256]{2,0,1:T(4,128)(2,1)} %copy.46), calls=%async_computation | async-start | bytes 131072 | tf_op jit(solution)/shard_map/all_to_all | solution.py:74
  45.7 6.8 %all-to-all-done = bf16[4,32,256]{2,0,1:T(4,128)(2,1)S(1)} async-done(((bf16[4,32,256]{2,0,1:T(4,128)(2,1)}), bf16[4,32,256]{2,0,1:T(4,128)(2,1)S(1)}, u32[]{:S(2)}, u32[]{:S(2)}) %all-to-all-start) | async-done | bytes 65568 | tf_op jit(solution)/shard_map/all_to_all | solution.py:74
  52.9 0.4 fusion.85
  53.5 4.7 %while.21 = (s32[]{:T(128)}, f32[8,2,64,32]{2,3,0,1:T(8,128)S(1)}, bf16[8,2,64,32]{2,3,0,1:T(8,128)(2,1)S(1)}, bf16[8,2,64,32]{2,3,0,1:T(8,128)(2,1)S(1)}, bf16[8,2,64,32]{2,3,0,1:T(8,128)(2,1)S(1)}, /*index=5*/s32[]{:T(128)}) while((s32[]{:T(128)}, f32[8,2,64,32]{2,3,0,1:T(8,128)S(1)}, bf16[8,2,64,32]{2,3,0,1:T(8,128)(2,1)S(1)}, ...), condition=%wide.region_13.14_spmd, body=%wide.region_10.13_spmd.sunk | while | flops 1614080 | bytes 119365 | solution.py:36
  53.5 0.2 fusion.168
  53.8 0.3 fusion.169
  54.1 0.2 fusion.168
  54.4 0.3 fusion.169
  54.7 0.2 fusion.168
  55.0 0.3 fusion.169
  55.3 0.2 fusion.168
  55.6 0.3 fusion.169
  55.9 0.2 fusion.168
  56.1 0.3 fusion.169
  56.5 0.2 fusion.168
  56.7 0.3 fusion.169
  57.1 0.2 fusion.168
  57.3 0.3 fusion.169
  57.7 0.2 fusion.168
  57.9 0.3 fusion.169
  58.4 0.3 convert_reduce_fusion.1
  58.7 0.2 fusion.105
  58.9 0.2 convolution_convert_fusion
  59.2 0.9 %reshape.131 = bf16[16,2,2048]{2,1,0:T(2,128)(2,1)} reshape(bf16[16,2,32,64]{3,2,1,0:T(8,128)(2,1)S(1)} %broadcast_bitcast_fusion) | data formatting | bytes 262144
  60.1 3.5 %all-to-all-start.1 = ((bf16[16,2,2048]{2,1,0:T(2,128)(2,1)}), bf16[16,2,2048]{2,1,0:T(2,128)(2,1)S(1)}, u32[]{:S(2)}, u32[]{:S(2)}) async-start(bf16[16,2,2048]{2,1,0:T(2,128)(2,1)} %reshape.131), calls=%async_computation.1 | async-start | bytes 262144 | tf_op jit(solution)/shard_map/all_to_all | solution.py:94
  63.6 0.7 copy.55
  64.3 7.2 %all-to-all-done.1 = bf16[16,2,2048]{2,1,0:T(2,128)(2,1)S(1)} async-done(((bf16[16,2,2048]{2,1,0:T(2,128)(2,1)}), bf16[16,2,2048]{2,1,0:T(2,128)(2,1)S(1)}, u32[]{:S(2)}, u32[]{:S(2)}) %all-to-all-start.1) | async-done | bytes 131104 | tf_op jit(solution)/shard_map/all_to_all | solution.py:94
  71.5 0.2 reshape.132
  71.7 0.3 fusion.72
  72.0 0.3 copy.54
  72.3 0.5 reshape.116
  72.8 0.8 %fusion.77 = bf16[2,32,128]{2,1,0:T(8,128)(2,1)} fusion(bf16[2,32,1024]{2,1,0:T(8,128)(2,1)S(1)} %reshape.116, bf16[1024,128]{1,0:T(8,128)(2,1)S(1)} %copy-done.3, bf16[2,32,128]{2,1,0:T(8,128)(2,1)S(1)} %copy-done.4), kind=kOutput, calls=%fused_computation.50 | convolution fusion | flops 16801792 | bytes 425984 | tf_op jit(solution)/shard_map/ijk,kz->ijz/dot_general | solution.py:100
  (52 shorter events, 1.1 us)
Async XLA Ops:
  0.6 2.0 %copy-start = (bf16[256,1024]{1,0:T(8,128)(2,1)S(1)}, bf16[256,1024]{1,0:T(8,128)(2,1)}, u32[]{:S(2)}) copy-start(bf16[256,1024]{1,0:T(8,128)(2,1)} %param.18) | copy-start | bytes 1572868
  7.1 4.4 %copy-start.4 = (bf16[2,32,128]{2,1,0:T(8,128)(2,1)S(1)}, bf16[2,32,128]{2,1,0:T(8,128)(2,1)}, u32[]{:S(2)}) copy-start(bf16[2,32,128]{2,1,0:T(8,128)(2,1)} %param.15) | copy-start | bytes 49156
  7.1 4.7 %copy-start.9 = (bf16[128,8]{0,1:T(8,128)(2,1)S(1)}, bf16[128,8]{0,1:T(8,128)(2,1)}, u32[]{:S(2)}) copy-start(bf16[128,8]{0,1:T(8,128)(2,1)} %param.17) | copy-start | bytes 6148
  35.4 5.9 %copy-start.7 = (s32[32,256]{1,0:T(8,128)S(1)}, s32[32,256]{1,0:T(8,128)}, u32[]{:S(2)}) copy-start(s32[32,256]{1,0:T(8,128)} %param.16) | copy-start | bytes 98308
  35.4 5.9 %copy-start.1 = (bf16[4,32,256]{2,1,0:T(8,128)(2,1)S(1)}, bf16[4,32,256]{2,1,0:T(8,128)(2,1)}, u32[]{:S(2)}) copy-start(bf16[4,32,256]{2,1,0:T(8,128)(2,1)} %param.14) | copy-start | bytes 196612
  35.4 5.9 %copy-start.6 = (bf16[256,256]{1,0:T(8,128)(2,1)S(1)}, bf16[256,256]{1,0:T(8,128)(2,1)}, u32[]{:S(2)}) copy-start(bf16[256,256]{1,0:T(8,128)(2,1)} %param.19) | copy-start | bytes 393220
  39.7 13.2 %copy-start.2 = (bf16[256,1024]{1,0:T(8,128)(2,1)S(1)}, bf16[256,1024]{1,0:T(8,128)(2,1)}, u32[]{:S(2)}) copy-start(bf16[256,1024]{1,0:T(8,128)(2,1)} %param.20) | copy-start | bytes 1572868
  42.2 10.4 %all-to-all-start = ((bf16[4,32,256]{2,0,1:T(4,128)(2,1)}), bf16[4,32,256]{2,0,1:T(4,128)(2,1)S(1)}, u32[]{:S(2)}, u32[]{:S(2)}) async-start(bf16[4,32,256]{2,0,1:T(4,128)(2,1)} %copy.46), calls=%async_computation | async-start | bytes 131072 | tf_op jit(solution)/shard_map/all_to_all | solution.py:74
  53.4 4.9 %copy-start.5 = (bf16[256,256]{1,0:T(8,128)(2,1)S(1)}, bf16[256,256]{1,0:T(8,128)(2,1)}, u32[]{:S(2)}) copy-start(bf16[256,256]{1,0:T(8,128)(2,1)} %param.21) | copy-start | bytes 393220
  53.4 5.4 %copy-start.8 = (bf16[256,64]{0,1:T(8,128)(2,1)S(1)}, bf16[256,64]{0,1:T(8,128)(2,1)}, u32[]{:S(2)}) copy-start(bf16[256,64]{0,1:T(8,128)(2,1)} %param.22) | copy-start | bytes 98308
  58.8 14.0 %copy-start.3 = (bf16[1024,128]{1,0:T(8,128)(2,1)S(1)}, bf16[1024,128]{1,0:T(8,128)(2,1)}, u32[]{:S(2)}) copy-start(bf16[1024,128]{1,0:T(8,128)(2,1)} %param.23) | copy-start | bytes 786436
  60.1 11.4 %all-to-all-start.1 = ((bf16[16,2,2048]{2,1,0:T(2,128)(2,1)}), bf16[16,2,2048]{2,1,0:T(2,128)(2,1)S(1)}, u32[]{:S(2)}, u32[]{:S(2)}) async-start(bf16[16,2,2048]{2,1,0:T(2,128)(2,1)} %reshape.131), calls=%async_computation.1 | async-start | bytes 262144 | tf_op jit(solution)/shard_map/all_to_all | solution.py:94
